TPU v7x, 32 devices: a whole 2x2x4 slice. The times are simulated.
32 devices in a mesh: dp: 16 (over z, y, core), mp: 2 (over x).
Axes of the slice: x: 2, y: 2, z: 4, core: 2. Of those that a mesh axis runs over, the one named last changes fastest.
Arguments:
- layer_input: bfloat16 [2, 16, 256, 2048], P(None, 'dp', 'mp')
- out_grad: bfloat16 [2, 16, 256, 2048], P(None, 'dp', 'mp')
- valid_count: int32 [2, 16], P(None, 'dp'), may hold values from 129 to 256, as said below
- w_query: bfloat16 [2048, 2048], P('dp', 'mp'), may hold values from -0.125 to 0.125
- w_key: bfloat16 [2048, 2048], P('dp', 'mp'), may hold values from -0.125 to 0.125
- w_value: bfloat16 [2048, 2048], P('dp', 'mp'), may hold values from -0.125 to 0.125
- w_output: bfloat16 [2048, 2048], P('dp', 'mp'), may hold values from -0.75 to 0.75
- w_gate: bfloat16 [2048, 8192], P('dp', 'mp'), may hold values from -0.125 to 0.125
- w_up: bfloat16 [2048, 8192], P('dp', 'mp'), may hold values from -0.125 to 0.125
- w_down: bfloat16 [2048, 8192], P('dp', 'mp'), may hold values from -0.0625 to 0.0625
- gain_attn: float32 [2048], replicated, may hold values from 0.5 to 1.5
- gain_mlp: float32 [2048], replicated, may hold values from 0.5 to 1.5
- memory_gate: float32 [16], replicated, may hold values from -3 to 3
Outputs:
- layer_output: bfloat16 [2, 16, 256, 2048], P(None, 'dp', 'mp')
- grad_input: float32 [2, 16, 256, 2048], P(None, 'dp', 'mp')
- grad_query: float32 [2048, 2048], P('dp', 'mp')
- grad_key: float32 [2048, 2048], P('dp', 'mp')
- grad_value: float32 [2048, 2048], P('dp', 'mp')
- grad_output: float32 [2048, 2048], P('dp', 'mp')
- grad_gate: float32 [2048, 8192], P('dp', 'mp')
- grad_up: float32 [2048, 8192], P('dp', 'mp')
- grad_down: float32 [2048, 8192], P('dp', 'mp')
- grad_norm_attn: float32 [2048], replicated
- grad_norm_mlp: float32 [2048], replicated
- grad_memory_gate: float32 [16], replicated
Inputs may be any that keep to these rules, and one draw needn't show every extreme that they name: valid_count counts the valid leading tokens of each sequence; its first segment is always full and some sequence is full to 256.
All inputs are finite; a program needn't handle non-finite values.
Results may differ from a plain program's by a relative error of at most 0.014.
Values may be sent and summed in bfloat16 or wider, within the bound.
No kernel may reach another device: no remote copies, remote signals or barrier semaphores. Data moves between devices by JAX's collectives and lax.ppermute only.
A program may use at most 448 MiB of HBM per device.

v0:
```python
import jax
import jax.numpy as jnp
from jax import lax
from jax.sharding import PartitionSpec as P

HD = 128
epsilon = 1e-05
masked_score = -1e30


def positive_map(values):
    return jnp.where(values > 0.0, values + 1.0, jnp.exp(jnp.minimum(values, 0.0)))


def positive_slope(values):
    return jnp.where(values > 0.0, 1.0, jnp.exp(jnp.minimum(values, 0.0)))


def gather_rows(local_rows):
    return lax.all_gather(local_rows, "mp", axis=1, tiled=True)


def reduce_rows(partial_value):
    return lax.psum_scatter(partial_value, "mp", scatter_dimension=1, tiled=True)


def fold_weights(inputs, weight):
    return jnp.dot(inputs, weight, preferred_element_type=jnp.float32)


def map_weights(inputs, weight):
    return lax.dot_general(
        inputs, weight, (((1,), (1,)), ((), ())), preferred_element_type=jnp.float32
    )


def make_term(pairs_list):
    columns = []
    for index in range(4):
        total = None
        for pairs in pairs_list:
            left_part = pairs[index][0]
            addend = lax.dot_general(
                left_part,
                pairs[index][1],
                (((0,), (0,)), ((), ())),
                preferred_element_type=jnp.float32,
            )
            total = addend if total is None else total + addend
        columns.append(total)
    return jnp.concatenate(columns, axis=1)


def run_block(
    local_in, local_grad, counts, w_qkv, w_output, w_gu, w_down, gain_attn, gain_mlp, gate_local
):
    seq_count, rows_local, width = local_in.shape
    full_len = rows_local * lax.axis_size("mp")
    seg_len = full_len // 2
    heads_local = gate_local.shape[0]
    attn_width = heads_local * HD
    ff_width = w_down.shape[1]
    total_rows = seq_count * full_len
    score_scale = HD ** (-0.5)
    shape_heads = (seq_count, 2, seg_len, heads_local, HD)
    valid_rows = (jnp.arange(full_len)[None, :] < counts[:, None]).astype(jnp.float32)
    inputs = local_in.astype(jnp.float32)
    inv_first = lax.rsqrt(jnp.mean(inputs * inputs, axis=-1, keepdims=True) + epsilon)
    normed = (inputs * inv_first * gain_attn).astype(jnp.bfloat16)
    normed_all = gather_rows(normed).reshape(total_rows, width)
    qkv_rows = fold_weights(normed_all, w_qkv).astype(jnp.bfloat16)
    queries = qkv_rows[:, :attn_width].reshape(shape_heads)
    key_rows = qkv_rows[:, attn_width : 2 * attn_width].reshape(shape_heads)
    value_rows = qkv_rows[:, 2 * attn_width :].reshape(shape_heads)
    raw_scores = (
        jnp.einsum("bnqhe,bnkhe->bnhqk", queries, key_rows, preferred_element_type=jnp.float32)
        * score_scale
    )
    seg_pos = jnp.arange(seg_len)
    causal = seg_pos[:, None] >= seg_pos[None, :]
    key_valid = valid_rows.reshape(seq_count, 2, 1, 1, seg_len) > 0.5
    scores = jnp.where(causal & key_valid, raw_scores, masked_score)
    top_score = jnp.max(scores, axis=-1, keepdims=True)
    exponent = jnp.exp(scores - top_score)
    probability = exponent / jnp.sum(exponent, axis=-1, keepdims=True)
    prob_low = probability.astype(jnp.bfloat16)
    local_out = jnp.einsum(
        "bnhqk,bnkhe->bnqhe", prob_low, value_rows, preferred_element_type=jnp.float32
    )
    query_map = positive_map(queries[:, 1].astype(jnp.float32)).astype(jnp.bfloat16)
    seg_valid = valid_rows[:, :seg_len].reshape(seq_count, seg_len, 1, 1)
    key_map = (
        positive_map(key_rows[:, 0].astype(jnp.float32)).astype(jnp.bfloat16).astype(jnp.float32)
        * seg_valid
    )
    key_map_low = key_map.astype(jnp.bfloat16)
    memory = jnp.einsum(
        "bthe,bthf->bhef", key_map_low, value_rows[:, 0], preferred_element_type=jnp.float32
    )
    memory_low = memory.astype(jnp.bfloat16)
    normalizer = jnp.sum(key_map, axis=1)
    numerator = jnp.einsum(
        "bthe,bhef->bthf", query_map, memory_low, preferred_element_type=jnp.float32
    )
    denominator = jnp.sum(query_map.astype(jnp.float32) * normalizer[:, None], axis=-1)
    retrieved = numerator / denominator[..., None]
    gate_sig = jax.nn.sigmoid(gate_local)
    gate_value = gate_sig[:, None]
    first_seg = (1.0 - gate_value) * local_out[:, 0]
    second = gate_value * retrieved + (1.0 - gate_value) * local_out[:, 1]
    combined = jnp.stack([first_seg, second], axis=1).reshape(seq_count, full_len, attn_width)
    heads_out = (
        (combined * valid_rows[..., None]).astype(jnp.bfloat16).reshape(total_rows, attn_width)
    )
    attn_out = reduce_rows(map_weights(heads_out, w_output).reshape(seq_count, full_len, width))
    hidden_state = inputs + attn_out
    inv_second = lax.rsqrt(jnp.mean(hidden_state * hidden_state, axis=-1, keepdims=True) + epsilon)
    normed_mlp = (hidden_state * inv_second * gain_mlp).astype(jnp.bfloat16)
    mlp_in = gather_rows(normed_mlp).reshape(total_rows, width)
    gate_up = fold_weights(mlp_in, w_gu)
    gate_pre = gate_up[:, :ff_width]
    up_pre = gate_up[:, ff_width:]
    sigma = jax.nn.sigmoid(gate_pre)
    activated = (gate_pre * sigma * up_pre).astype(jnp.bfloat16)
    mlp_out = reduce_rows(map_weights(activated, w_down).reshape(seq_count, full_len, width))
    layer_out = (hidden_state + mlp_out).astype(jnp.bfloat16)
    grad_rows = gather_rows(local_grad).reshape(total_rows, width)
    act_back = fold_weights(grad_rows, w_down)
    gate_back = (act_back * up_pre * sigma * (1.0 + gate_pre * (1.0 - sigma))).astype(jnp.bfloat16)
    up_back = (act_back * gate_pre * sigma).astype(jnp.bfloat16)
    grad_gu = jnp.concatenate([gate_back, up_back], axis=1)
    mlp_back = reduce_rows(map_weights(grad_gu, w_gu).reshape(seq_count, full_len, width))
    scaled_mlp = mlp_back * gain_mlp
    hidden_back = local_grad.astype(jnp.float32) + inv_second * (
        scaled_mlp
        - hidden_state
        * inv_second
        * inv_second
        * jnp.mean(scaled_mlp * hidden_state, axis=-1, keepdims=True)
    )
    gain_mlp_part = jnp.sum(mlp_back * hidden_state * inv_second, axis=(0, 1))
    hidden_rows = gather_rows(hidden_back.astype(jnp.bfloat16)).reshape(total_rows, width)
    heads_grad = fold_weights(hidden_rows, w_output)
    grad_comb = (
        heads_grad.reshape(seq_count, full_len, attn_width) * valid_rows[..., None]
    ).reshape(shape_heads)
    gate_sum = jnp.sum(
        grad_comb[:, 0] * -local_out[:, 0] + grad_comb[:, 1] * (retrieved - local_out[:, 1]),
        axis=(0, 1, 3),
    )
    gate_part = gate_sum * gate_sig * (1.0 - gate_sig)
    local_back = ((1.0 - gate_value) * grad_comb).astype(jnp.bfloat16)
    retrieved_back = gate_value * grad_comb[:, 1]
    numer_back = (retrieved_back / denominator[..., None]).astype(jnp.bfloat16)
    denom_back = -jnp.sum(retrieved_back * numerator, axis=-1) / (denominator * denominator)
    prob_back = jnp.einsum(
        "bnqhe,bnkhe->bnhqk", local_back, value_rows, preferred_element_type=jnp.float32
    )
    value_back = jnp.einsum(
        "bnhqk,bnqhe->bnkhe", prob_low, local_back, preferred_element_type=jnp.float32
    )
    score_back = (
        probability * (prob_back - jnp.sum(prob_back * probability, axis=-1, keepdims=True))
    ).astype(jnp.bfloat16)
    query_back = (
        jnp.einsum("bnhqk,bnkhe->bnqhe", score_back, key_rows, preferred_element_type=jnp.float32)
        * score_scale
    )
    key_back = (
        jnp.einsum("bnhqk,bnqhe->bnkhe", score_back, queries, preferred_element_type=jnp.float32)
        * score_scale
    )
    memory_back = jnp.einsum(
        "bthe,bthf->bhef", query_map, numer_back, preferred_element_type=jnp.float32
    ).astype(jnp.bfloat16)
    qmap_back = (
        jnp.einsum("bthf,bhef->bthe", numer_back, memory_low, preferred_element_type=jnp.float32)
        + denom_back[..., None] * normalizer[:, None]
    )
    norm_back = jnp.sum(denom_back[..., None] * query_map.astype(jnp.float32), axis=1)
    kmap_back = (
        jnp.einsum(
            "bthf,bhef->bthe", value_rows[:, 0], memory_back, preferred_element_type=jnp.float32
        )
        + norm_back[:, None]
    ) * seg_valid
    value_from_memory = jnp.einsum(
        "bthe,bhef->bthf", key_map_low, memory_back, preferred_element_type=jnp.float32
    )
    query_back = query_back.at[:, 1].add(
        qmap_back * positive_slope(queries[:, 1].astype(jnp.float32))
    )
    key_back = key_back.at[:, 0].add(kmap_back * positive_slope(key_rows[:, 0].astype(jnp.float32)))
    value_back = value_back.at[:, 0].add(value_from_memory)
    grad_qkv = jnp.concatenate(
        [
            query_back.reshape(total_rows, attn_width).astype(jnp.bfloat16),
            key_back.reshape(total_rows, attn_width).astype(jnp.bfloat16),
            value_back.reshape(total_rows, attn_width).astype(jnp.bfloat16),
        ],
        axis=1,
    )
    attn_back = reduce_rows(map_weights(grad_qkv, w_qkv).reshape(seq_count, full_len, width))
    scaled_attn = attn_back * gain_attn
    grad_input = hidden_back + inv_first * (
        scaled_attn
        - inputs * inv_first * inv_first * jnp.mean(scaled_attn * inputs, axis=-1, keepdims=True)
    )
    gain_attn_part = jnp.sum(attn_back * inputs * inv_first, axis=(0, 1))
    pairs = (
        (normed_all, grad_qkv),
        (hidden_rows, heads_out),
        (mlp_in, grad_gu),
        (grad_rows, activated),
    )
    return (layer_out, grad_input, pairs, gain_attn_part, gain_mlp_part, gate_part)


def on_device(
    layer_input,
    out_grad,
    valid_count,
    w_query,
    w_key,
    w_value,
    w_output,
    w_gate,
    w_up,
    w_down,
    gain_attn,
    gain_mlp,
    memory_gate,
):
    heads_local = w_query.shape[1] // HD
    head_start = lax.axis_index("mp") * heads_local
    gate_local = lax.dynamic_slice_in_dim(memory_gate, head_start, heads_local, 0)
    w_qkv_part = jnp.concatenate([w_query, w_key, w_value], axis=1)
    w_gu_part = jnp.concatenate([w_gate, w_up], axis=1)
    micro_count = layer_input.shape[0]
    outcomes = []
    for micro in range(micro_count):
        w_qkv, w_out_full, w_gu, w_down_full = (
            lax.all_gather(w_qkv_part, "dp", axis=0, tiled=True),
            lax.all_gather(w_output, "dp", axis=0, tiled=True),
            lax.all_gather(w_gu_part, "dp", axis=0, tiled=True),
            lax.all_gather(w_down, "dp", axis=0, tiled=True),
        )
        outcomes.append(
            run_block(
                layer_input[micro],
                out_grad[micro],
                valid_count[micro],
                w_qkv,
                w_out_full,
                w_gu,
                w_down_full,
                gain_attn,
                gain_mlp,
                gate_local,
            )
        )
    layer_output = jnp.stack([outcome[0] for outcome in outcomes], axis=0)
    grad_input = jnp.stack([outcome[1] for outcome in outcomes], axis=0)
    gain_attn_sum = outcomes[0][3]
    gain_mlp_sum = outcomes[0][4]
    gate_sum = outcomes[0][5]
    for outcome in outcomes[1:]:
        gain_attn_sum = gain_attn_sum + outcome[3]
        gain_mlp_sum = gain_mlp_sum + outcome[4]
        gate_sum = gate_sum + outcome[5]
    all_grads = lax.psum_scatter(
        make_term([outcome[2] for outcome in outcomes]), "dp", scatter_dimension=0, tiled=True
    )
    gate_full = lax.dynamic_update_slice_in_dim(
        jnp.zeros((memory_gate.shape[0],), jnp.float32), gate_sum, head_start, 0
    )
    grad_norm_attn, grad_norm_mlp, grad_memory_gate = lax.psum(
        (gain_attn_sum, gain_mlp_sum, gate_full), ("dp", "mp")
    )
    attn_width = w_query.shape[1]
    ff_width = w_gate.shape[1]
    grad_query = all_grads[:, :attn_width]
    grad_key = all_grads[:, attn_width : 2 * attn_width]
    grad_value = all_grads[:, 2 * attn_width : 3 * attn_width]
    grad_output = all_grads[:, 3 * attn_width : 4 * attn_width]
    mlp_start = 4 * attn_width
    grad_gate = all_grads[:, mlp_start : mlp_start + ff_width]
    grad_up = all_grads[:, mlp_start + ff_width : mlp_start + 2 * ff_width]
    grad_down = all_grads[:, mlp_start + 2 * ff_width :]
    return (
        layer_output,
        grad_input,
        grad_query,
        grad_key,
        grad_value,
        grad_output,
        grad_gate,
        grad_up,
        grad_down,
        grad_norm_attn,
        grad_norm_mlp,
        grad_memory_gate,
    )


def solution(mesh):
    in_specs = (
        P(None, "dp", "mp", None),
        P(None, "dp", "mp", None),
        P(None, "dp"),
        P("dp", "mp"),
        P("dp", "mp"),
        P("dp", "mp"),
        P("dp", "mp"),
        P("dp", "mp"),
        P("dp", "mp"),
        P("dp", "mp"),
        P(),
        P(),
        P(),
    )
    out_specs = (
        P(None, "dp", "mp", None),
        P(None, "dp", "mp", None),
        P("dp", "mp"),
        P("dp", "mp"),
        P("dp", "mp"),
        P("dp", "mp"),
        P("dp", "mp"),
        P("dp", "mp"),
        P("dp", "mp"),
        P(),
        P(),
        P(),
    )
    return jax.shard_map(
        on_device, mesh=mesh, in_specs=in_specs, out_specs=out_specs, check_vma=False
    )
```

profile of v0, /device:TPU:0, one launch (start us, length us, event | category | flops | bytes accessed | tf_op | source)
XLA Modules:
  0.0 2450.9 jit_solution(10534813084720500561)
XLA Ops:
  19.5 16.5 all-gather.27.cloned.1.call-done
  36.0 103.3 %all-gather.17.cloned.1.call-done = bf16[2048,3072]{1,0:T(8,128)(2,1)} async-done(((bf16[128,3072]{1,0:T(8,128)(2,1)}), bf16[2048,3072]{1,0:T(8,128)(2,1)}) %all-gather.17.cloned.1.call-update) | async-done | bytes 12582928 | tf_op jit(solution)/shard_map/all_gather | solution.py:243
  190.0 23.5 all-gather.19.cloned.1.call-done
  225.6 23.4 reduce-scatter.14.cloned.1.call-done
  249.0 34.6 %reduce-scatter.10.cloned.1.call-done = f32[1,128,2048]{2,1,0:T(8,128)} async-done(((f32[1,256,2048]{2,1,0:T(8,128)}), f32[1,128,2048]{2,1,0:T(8,128)}) %reduce-scatter.10.cloned.1.call-update) | async-done | bytes 1048592 | tf_op jit(solution)/shard_map/reduce_scatter | solution.py:24
  291.7 16.3 all-gather.21.cloned.1.call-done
  308.0 170.2 %all-gather.23.cloned.1.call-done = bf16[2048,8192]{1,0:T(8,128)(2,1)} async-done(((bf16[128,8192]{1,0:T(8,128)(2,1)}), bf16[2048,8192]{1,0:T(8,128)(2,1)}) %all-gather.23.cloned.1.call-update) | async-done | bytes 33554448 | tf_op jit(solution)/shard_map/all_gather | solution.py:245
  478.2 17.9 fusion.87
  501.6 128.5 %all-gather.25.cloned.1.call-done = bf16[2048,4096]{1,0:T(8,128)(2,1)} async-done(((bf16[128,4096]{1,0:T(8,128)(2,1)}), bf16[2048,4096]{1,0:T(8,128)(2,1)}) %all-gather.25.cloned.1.call-update) | async-done | bytes 16777232 | tf_op jit(solution)/shard_map/all_gather | solution.py:246
  643.3 17.2 convolution_bitcast_fusion.3
  660.6 30.1 %reduce-scatter.18.cloned.1.call-done = f32[1,128,2048]{2,1,0:T(8,128)} async-done(((f32[1,256,2048]{2,1,0:T(8,128)}), f32[1,128,2048]{2,1,0:T(8,128)}) %reduce-scatter.18.cloned.1.call-update) | async-done | bytes 1048592 | tf_op jit(solution)/shard_map/reduce_scatter | solution.py:24
  694.9 20.3 all-gather.29.cloned.1.call-done
  715.2 17.9 fusion.82
  751.2 17.2 convolution_bitcast_fusion.1
  781.2 19.3 reduce-scatter.22.cloned.1.call-done
  802.6 31.9 %reduce-scatter.16.cloned.1.call-done = f32[1,128,2048]{2,1,0:T(8,128)} async-done(((f32[1,256,2048]{2,1,0:T(8,128)}), f32[1,128,2048]{2,1,0:T(8,128)}) %reduce-scatter.16.cloned.1.call-update) | async-done | bytes 1048592 | tf_op jit(solution)/shard_map/reduce_scatter | solution.py:24
  839.0 20.6 all-gather.33.cloned.1.call-done
  964.6 26.6 %fusion.2 = f32[2048,8192]{1,0:T(8,128)} fusion(bf16[256,4096]{1,0:T(8,128)(2,1)} %get-tuple-element.110, bf16[256,4096]{1,0:T(8,128)(2,1)} %get-tuple-element.109, bf16[1,256,2048]{2,1,0:T(8,128)(2,1)} %all-gather.21.cloned.1.call-done), kind=kOutput, calls=%fused_computation.27 | convolution fusion | flops 8598323200 | bytes 72351744 | tf_op jit(solution)/shard_map/dot_general | solution.py:43
  991.2 26.6 %add_bitcast_fusion = f32[2048,4096]{1,0:T(8,128)} fusion(f32[4096,2048]{0,1:T(8,128)} %fusion.77, bf16[256,4096]{1,0:T(8,128)(2,1)} %get-tuple-element.121, bf16[1,1,256,2048]{3,2,1,0:T(8,128)(2,1)} %all-gather.37.cloned.1.call-done), kind=kOutput, calls=%fused_computation.4 | convolution fusion | flops 4303355904 | bytes 70254592 | tf_op jit(solution)/shard_map/dot_general | solution.py:43
  1017.7 47.7 %convolution_add_fusion = f32[2048,8192]{1,0:T(8,128)} fusion(f32[2048,8192]{1,0:T(8,128)} %fusion.2, bf16[256,4096]{1,0:T(8,128)(2,1)} %get-tuple-element.112, bf16[256,4096]{1,0:T(8,128)(2,1)S(1)} %copy-done.39, bf16[1,256,2048]{2,1,0:T(8,128)(2,1)} %all-gather.29.cloned.1.call-done), kind=kOutput, calls=%fused_computation.3 | convolution fusion | flops 8615100416 | bytes 139460608 | tf_op jit(solution)/shard_map/dot_general | solution.py:43
  1093.7 16.8 convolution_add_fusion.1
  1110.5 86.1 %pad_maximum_fusion = f32[2048,16384]{1,0:T(8,128)} fusion(f32[2048,4096]{1,0:T(8,128)} %add_bitcast_fusion, f32[2048,8192]{1,0:T(8,128)} %convolution_add_fusion, f32[2048,1024]{1,0:T(8,128)} %copy.140, f32[2048,3072]{1,0:T(8,128)} %convolution_add_fusion.1), kind=kLoop, calls=%fused_computation.2 | loop fusion | flops 100663296 | bytes 268435456 | tf_op jit(solution)/shard_map/concatenate | solution.py:51
  1200.0 39.8 %all-reduce = (f32[2048]{0:T(1024)}, f32[2048]{0:T(1024)}, f32[16]{0:T(128)}) all-reduce(f32[2048]{0:T(1024)S(1)} %add.328, f32[2048]{0:T(1024)S(1)} %add.329, f32[16]{0:T(128)S(1)} %fusion.166), channel_id=1, replica_groups=mesh['dp'=16,'mp'=2] {'dp','mp'}, use_global_device_ids=true, to_apply=%region_33.34 | all-reduce | flops 4112 | bytes 32896 | tf_op jit(solution)/shard_map/psum | solution.py:277
  1247.4 1187.8 %reduce-scatter.26.cloned.1.call-done = f32[128,16384]{1,0:T(8,128)} async-done(((f32[2048,16384]{1,0:T(8,128)}), f32[128,16384]{1,0:T(8,128)}) %reduce-scatter.26.cloned.1.call-update) | async-done | bytes 8388624 | tf_op jit(solution)/shard_map/reduce_scatter | solution.py:271
  (397 shorter events, 294.8 us)
Async XLA Ops:
  7.2 28.8 %all-gather.27.cloned.1.call-start = ((), (), s32[]{:S(2)}) async-start(), calls=%async_computation.17 | async-start | bytes 1572864 | tf_op jit(solution)/shard_map/all_gather | solution.py:20
  11.8 127.5 %all-gather.17.cloned.1.call-start = ((), (), s32[]{:S(2)}) async-start(), calls=%async_computation.10 | async-start | bytes 13369344 | tf_op jit(solution)/shard_map/all_gather | solution.py:243
  13.9 147.1 %all-gather.15.cloned.1.call-start = ((), (), s32[]{:S(2)}) async-start(), calls=%async_computation.9 | async-start | bytes 1572864 | tf_op jit(solution)/shard_map/all_gather | solution.py:20
  14.7 198.8 %all-gather.19.cloned.1.call-start = ((), (), s32[]{:S(2)}) async-start(), calls=%async_computation.11 | async-start | bytes 4456448 | tf_op jit(solution)/shard_map/all_gather | solution.py:244
  15.3 233.7 %reduce-scatter.14.cloned.1.call-start = ((), (), s32[]{:S(2)}) async-start(), calls=%async_computation.18 | async-start | bytes 3145728 | tf_op jit(solution)/shard_map/reduce_scatter | solution.py:24
  18.0 907.8 %copy-start.74 = (f32[8]{0:T(128)}, f32[8]{0:T(128)S(1)}, u32[]{:S(2)}) copy-start(f32[8]{0:T(128)S(1)} %get-tuple-element.108) | copy-start | bytes 100
  218.4 65.2 %reduce-scatter.10.cloned.1.call-start = ((), (), s32[]{:S(2)}) async-start(), calls=%async_computation.12 | async-start | bytes 3145728 | tf_op jit(solution)/shard_map/reduce_scatter | solution.py:24
  225.5 82.4 %all-gather.21.cloned.1.call-start = ((), (), s32[]{:S(2)}) async-start(), calls=%async_computation.13 | async-start | bytes 1572864 | tf_op jit(solution)/shard_map/all_gather | solution.py:20
  285.5 549.0 %copy-start = (f32[1,128,2048]{2,1,0:T(8,128)}, f32[1,128,2048]{2,1,0:T(8,128)S(1)}, u32[]{:S(2)}) copy-start(f32[1,128,2048]{2,1,0:T(8,128)S(1)} %get-tuple-element.146) | copy-start | bytes 3145732
  285.5 549.0 %copy-start.2 = (f32[1,128,2048]{2,1,0:T(8,128)}, f32[1,128,2048]{2,1,0:T(8,128)S(1)}, u32[]{:S(2)}) copy-start(f32[1,128,2048]{2,1,0:T(8,128)S(1)} %get-tuple-element.104) | copy-start | bytes 3145732
  286.5 191.7 %all-gather.23.cloned.1.call-start = ((), (), s32[]{:S(2)}) async-start(), calls=%async_computation.14 | async-start | bytes 35651584 | tf_op jit(solution)/shard_map/all_gather | solution.py:245
  289.9 211.8 %all-gather.35.cloned.1.call-start = ((), (), s32[]{:S(2)}) async-start(), calls=%async_computation.28 | async-start | bytes 1572864 | tf_op jit(solution)/shard_map/all_gather | solution.py:20
  291.0 339.1 %all-gather.25.cloned.1.call-start = ((), (), s32[]{:S(2)}) async-start(), calls=%async_computation.15 | async-start | bytes 17825792 | tf_op jit(solution)/shard_map/all_gather | solution.py:246
  291.6 399.1 %reduce-scatter.18.cloned.1.call-start = ((), (), s32[]{:S(2)}) async-start(), calls=%async_computation.21 | async-start | bytes 3145728 | tf_op jit(solution)/shard_map/reduce_scatter | solution.py:24
  660.5 54.7 %all-gather.29.cloned.1.call-start = ((), (), s32[]{:S(2)}) async-start(), calls=%async_computation.19 | async-start | bytes 1572864 | tf_op jit(solution)/shard_map/all_gather | solution.py:20
  693.7 44.3 %all-gather.37.cloned.1.call-start = ((), (), s32[]{:S(2)}) async-start(), calls=%async_computation.29 | async-start | bytes 1572864 | tf_op jit(solution)/shard_map/all_gather | solution.py:20
  694.4 106.0 %reduce-scatter.22.cloned.1.call-start = ((), (), s32[]{:S(2)}) async-start(), calls=%async_computation.24 | async-start | bytes 3145728 | tf_op jit(solution)/shard_map/reduce_scatter | solution.py:24
  768.4 66.1 %reduce-scatter.16.cloned.1.call-start = ((), (), s32[]{:S(2)}) async-start(), calls=%async_computation.20 | async-start | bytes 3145728 | tf_op jit(solution)/shard_map/reduce_scatter | solution.py:24
  781.1 78.5 %all-gather.33.cloned.1.call-start = ((), (), s32[]{:S(2)}) async-start(), calls=%async_computation.25 | async-start | bytes 1572864 | tf_op jit(solution)/shard_map/all_gather | solution.py:20
  838.1 44.1 %all-gather.31.cloned.1.call-start = ((), (), s32[]{:S(2)}) async-start(), calls=%async_computation.22 | async-start | bytes 1572864 | tf_op jit(solution)/shard_map/all_gather | solution.py:20
  838.8 358.7 %reduce-scatter.24.cloned.1.call-start = ((), (), s32[]{:S(2)}) async-start(), calls=%async_computation.26 | async-start | bytes 3145728 | tf_op jit(solution)/shard_map/reduce_scatter | solution.py:24
  917.3 280.2 %reduce-scatter.20.cloned.1.call-start = ((), (), s32[]{:S(2)}) async-start(), calls=%async_computation.23 | async-start | bytes 3145728 | tf_op jit(solution)/shard_map/reduce_scatter | solution.py:24
  937.7 302.1 %reduce-scatter.12.cloned.1.call-start = ((), (), s32[]{:S(2)}) async-start(), calls=%async_computation.16 | async-start | bytes 3145728 | tf_op jit(solution)/shard_map/reduce_scatter | solution.py:24
  949.1 1486.1 %reduce-scatter.26.cloned.1.call-start = ((), (), s32[]{:S(2)}) async-start(), calls=%async_computation.27 | async-start | bytes 142606336 | tf_op jit(solution)/shard_map/reduce_scatter | solution.py:271
  (97 other events, 1984.8 us)
Sparse Core Ops, SparseCore 0:
  11.9 24.0 all-gather.26
  38.8 100.4 all-gather.16
  141.4 19.5 all-gather.14
  163.0 50.3 all-gather.18
  218.5 30.4 reduce-scatter.13
  251.6 31.9 reduce-scatter.9
  286.7 21.2 all-gather.20
  310.1 168.0 all-gather.22
  480.3 21.2 all-gather.34
  503.6 126.4 all-gather.24
  660.6 30.0 reduce-scatter.17
  693.8 21.2 all-gather.28
  716.7 21.2 all-gather.36
  768.5 31.8 reduce-scatter.21
  802.6 31.8 reduce-scatter.15
  838.3 21.2 all-gather.32
  861.0 21.2 all-gather.30
  917.4 31.8 reduce-scatter.23
  951.6 31.9 reduce-scatter.19
  986.2 31.8 reduce-scatter.11
  1196.9 1238.2 reduce-scatter.25
where the time goes:
time: 2460 us; the launch traced here: 2450 us
  waiting for transfers between devices  1860 us (76%)
  matrix products  345 us (14%)
  other arithmetic  132 us (5%)
  local copies, waits for them, and re-layouts  55.9 us (2%)
  blocking collectives  39.8 us (2%)
    reduce_scatter x1, waiting for transfers between devices, on_device(): lax.psum_scatter(make_term([outcome[2] for outcome in outcomes]), 'dp', s...  1190 us
    all_gather x1, waiting for transfers between devices, on_device(): lax.all_gather(w_gu_part, 'dp', axis=0, tiled=True)  170 us
    dot_general x8, matrix products, make_term(): lax.dot_general(left_part, pairs[index][1], (((0,), (0,)), ((), ())), pre...  151 us
    reduce_scatter x8, waiting for transfers between devices, reduce_rows(): lax.psum_scatter(partial_value, 'mp', scatter_dimension=1, tiled=True)  139 us
    all_gather x1, waiting for transfers between devices, on_device(): lax.all_gather(w_down, 'dp', axis=0, tiled=True)  128 us
    all_gather x1, waiting for transfers between devices, on_device(): lax.all_gather(w_qkv_part, 'dp', axis=0, tiled=True)  103 us
    all_gather x8, waiting for transfers between devices, gather_rows(): return lax.all_gather(local_rows, 'mp', axis=1, tiled=True)  103 us
    dot_general x8, matrix products, fold_weights(): return jnp.dot(inputs, weight, preferred_element_type=jnp.float32)  86.2 us
  transfers between devices with their start and end apart: 21, of which 18 were waited for; matrix products, arithmetic and copies ran while one was open for 17% of the time, Pallas kernels for 0%

commit v1 on v0

--- a/solution.py
+++ b/solution.py
@@ -17,7 +17,26 @@
 
 
 def gather_rows(local_rows):
-    return lax.all_gather(local_rows, "mp", axis=1, tiled=True)
+
+    def trace_knots(my_data, row_axis):
+        mid_arr = lax.psum(1, row_axis)
+        g_now, clean, later = (mid_arr, lax.axis_index(row_axis), my_data.shape[1])
+        now, e_now = (my_data, 1)
+        while e_now < g_now:
+            now = jnp.concatenate(
+                [
+                    now,
+                    lax.ppermute(
+                        now, row_axis, [(num, (num - e_now) % g_now) for num in range(g_now)]
+                    ),
+                ],
+                axis=1,
+            )
+            e_now = 2 * e_now
+        t1 = jnp.roll(now, shift=clean * later, axis=1)
+        return t1
+
+    return trace_knots(local_rows, "mp")
 
 
 def reduce_rows(partial_value):

time: 2460 us -> 2350 us (0.955)
  waiting for transfers between devices: 1860 us -> 1710 us
    all_gather x8 -> x0, waiting for transfers between devices: 103 us -> none  [gather_rows(): return lax.all_gather(local_rows, 'mp', axis=1, tiled=True)]
    ppermute x0 -> x8, waiting for transfers between devices: none -> 37.8 us  [trace_knots(): lax.ppermute(now, row_axis, [(num, (num - e_now) % g_now) for num in rang...]
    all_gather x1, waiting for transfers between devices: 103 us -> 74.4 us  [on_device(): lax.all_gather(w_qkv_part, 'dp', axis=0, tiled=True)]
  transfers between devices with their start and end apart: 21 -> 21, of which waited for: 18 -> 13; matrix products, arithmetic and copies ran while one was open for 17% -> 17% of each run, Pallas kernels for 0% -> 0%
where the time goes in v1:
time: 2350 us; the launch traced here: 2330 us
  waiting for transfers between devices  1710 us (73%)
  matrix products  340 us (14%)
  other arithmetic  146 us (6%)
  local copies, waits for them, and re-layouts  76.3 us (3%)
  blocking collectives  40 us (2%)
    reduce_scatter x1, waiting for transfers between devices, on_device(): lax.psum_scatter(make_term([outcome[2] for outcome in outcomes]), 'dp', s...  1190 us
    all_gather x1, waiting for transfers between devices, on_device(): lax.all_gather(w_gu_part, 'dp', axis=0, tiled=True)  152 us
    reduce_scatter x8, waiting for transfers between devices, reduce_rows(): lax.psum_scatter(partial_value, 'mp', scatter_dimension=1, tiled=True)  143 us
    dot_general x8, matrix products, make_term(): lax.dot_general(left_part, pairs[index][1], (((0,), (0,)), ((), ())), pre...  140 us
    all_gather x1, waiting for transfers between devices, on_device(): lax.all_gather(w_down, 'dp', axis=0, tiled=True)  110 us
    dot_general x8, matrix products, fold_weights(): return jnp.dot(inputs, weight, preferred_element_type=jnp.float32)  88.4 us
    concatenate x1, other arithmetic, make_term(): return jnp.concatenate(columns, axis=1)  86.1 us
    dot_general x8, matrix products, map_weights(): lax.dot_general(inputs, weight, (((1,), (1,)), ((), ())), preferred_eleme...  85.6 us
  transfers between devices with their start and end apart: 21, of which 13 were waited for; matrix products, arithmetic and copies ran while one was open for 17% of the time, Pallas kernels for 0%

profile of v1, /device:TPU:0, one launch (start us, length us, event | category | flops | bytes accessed | tf_op | source)
XLA Modules:
  0.0 2334.9 jit_solution(7170223940809669042)
XLA Ops:
  39.6 74.4 %all-gather.5.cloned.1.call-done = bf16[2048,3072]{1,0:T(8,128)(2,1)} async-done(((bf16[128,3072]{1,0:T(8,128)(2,1)}), bf16[2048,3072]{1,0:T(8,128)(2,1)}) %all-gather.5.cloned.1.call-update) | async-done | bytes 12582928 | tf_op jit(solution)/shard_map/all_gather | solution.py:262
  184.7 27.4 %reduce-scatter.14.cloned.1.call-done = f32[1,128,2048]{2,1,0:T(8,128)} async-done(((f32[1,256,2048]{2,1,0:T(8,128)}), f32[1,128,2048]{2,1,0:T(8,128)}) %reduce-scatter.14.cloned.1.call-update) | async-done | bytes 1048592 | tf_op jit(solution)/shard_map/reduce_scatter | solution.py:43
  212.1 34.6 %reduce-scatter.10.cloned.1.call-done = f32[1,128,2048]{2,1,0:T(8,128)} async-done(((f32[1,256,2048]{2,1,0:T(8,128)}), f32[1,128,2048]{2,1,0:T(8,128)}) %reduce-scatter.10.cloned.1.call-update) | async-done | bytes 1048592 | tf_op jit(solution)/shard_map/reduce_scatter | solution.py:43
  265.1 151.7 %all-gather.9.cloned.1.call-done = bf16[2048,8192]{1,0:T(8,128)(2,1)} async-done(((bf16[128,8192]{1,0:T(8,128)(2,1)}), bf16[2048,8192]{1,0:T(8,128)(2,1)}) %all-gather.9.cloned.1.call-update) | async-done | bytes 33554448 | tf_op jit(solution)/shard_map/all_gather | solution.py:264
  416.7 18.8 fusion.202
  435.6 109.6 %all-gather.11.cloned.1.call-done = bf16[2048,4096]{1,0:T(8,128)(2,1)} async-done(((bf16[128,4096]{1,0:T(8,128)(2,1)}), bf16[2048,4096]{1,0:T(8,128)(2,1)}) %all-gather.11.cloned.1.call-update) | async-done | bytes 16777232 | tf_op jit(solution)/shard_map/all_gather | solution.py:265
  545.2 15.7 multiply_convert_fusion.3
  560.9 17.2 convolution_bitcast_fusion.3
  580.6 36.6 %reduce-scatter.18.cloned.1.call-done = f32[1,128,2048]{2,1,0:T(8,128)} async-done(((f32[1,256,2048]{2,1,0:T(8,128)}), f32[1,128,2048]{2,1,0:T(8,128)}) %reduce-scatter.18.cloned.1.call-update) | async-done | bytes 1048592 | tf_op jit(solution)/shard_map/reduce_scatter | solution.py:43
  635.0 17.5 fusion.203
  652.4 15.7 multiply_convert_fusion.1
  668.2 17.2 convolution_bitcast_fusion.1
  685.7 13.0 convolution_bitcast_fusion.4
  703.0 12.6 reduce-scatter.22.cloned.1.call-done
  717.7 32.1 %reduce-scatter.16.cloned.1.call-done = f32[1,128,2048]{2,1,0:T(8,128)} async-done(((f32[1,256,2048]{2,1,0:T(8,128)}), f32[1,128,2048]{2,1,0:T(8,128)}) %reduce-scatter.16.cloned.1.call-update) | async-done | bytes 1048592 | tf_op jit(solution)/shard_map/reduce_scatter | solution.py:43
  753.8 13.7 fusion.205
  845.7 12.4 convolution_bitcast_fusion.5
  858.1 25.6 %fusion.2 = f32[2048,8192]{1,0:T(8,128)} fusion(bf16[256,2048]{1,0:T(8,128)(2,1)S(1)} %copy-done.28, bf16[256,4096]{1,0:T(8,128)(2,1)} %get-tuple-element.111, bf16[256,4096]{1,0:T(8,128)(2,1)} %get-tuple-element.110), kind=kOutput, calls=%fused_computation.27 | convolution fusion | flops 8598323200 | bytes 72351744 | tf_op jit(solution)/shard_map/dot_general | solution.py:62
  884.9 22.3 convolution_add_fusion.1
  907.2 44.1 %convolution_add_fusion = f32[2048,8192]{1,0:T(8,128)} fusion(f32[2048,8192]{1,0:T(8,128)} %fusion.2, bf16[256,2048]{1,0:T(8,128)(2,1)S(1)} %copy-done.32, bf16[256,4096]{1,0:T(8,128)(2,1)} %get-tuple-element.113, bf16[256,4096]{1,0:T(8,128)(2,1)} %get-tuple-element.112), kind=kOutput, calls=%fused_computation.3 | convolution fusion | flops 8615100416 | bytes 139460608 | tf_op jit(solution)/shard_map/dot_general | solution.py:62
  978.5 16.5 convolution_add_fusion.2
  995.0 86.1 %pad_maximum_fusion = f32[2048,16384]{1,0:T(8,128)} fusion(f32[2048,4096]{1,0:T(8,128)} %convolution_add_fusion.1, f32[2048,8192]{1,0:T(8,128)} %convolution_add_fusion, f32[2048,1024]{1,0:T(8,128)} %copy.136, f32[2048,3072]{1,0:T(8,128)} %convolution_add_fusion.2), kind=kLoop, calls=%fused_computation.2 | loop fusion | flops 100663296 | bytes 268435456 | tf_op jit(solution)/shard_map/concatenate | solution.py:70
  1084.5 40.0 %all-reduce = (f32[2048]{0:T(1024)}, f32[2048]{0:T(1024)}, f32[16]{0:T(128)}) all-reduce(f32[2048]{0:T(1024)S(1)} %add.332, f32[2048]{0:T(1024)S(1)} %add.333, f32[16]{0:T(128)S(1)} %fusion.176), channel_id=1, replica_groups=mesh['dp'=16,'mp'=2] {'dp','mp'}, use_global_device_ids=true, to_apply=%region_33.35 | all-reduce | flops 4112 | bytes 32896 | tf_op jit(solution)/shard_map/psum | solution.py:296
  1132.2 1187.1 %reduce-scatter.26.cloned.1.call-done = f32[128,16384]{1,0:T(8,128)} async-done(((f32[2048,16384]{1,0:T(8,128)}), f32[128,16384]{1,0:T(8,128)}) %reduce-scatter.26.cloned.1.call-update) | async-done | bytes 8388624 | tf_op jit(solution)/shard_map/reduce_scatter | solution.py:290
  (461 shorter events, 277.1 us)
Async XLA Ops:
  7.2 106.9 %all-gather.5.cloned.1.call-start = ((), (), s32[]{:S(2)}) async-start(), calls=%async_computation.9 | async-start | bytes 13369344 | tf_op jit(solution)/shard_map/all_gather | solution.py:262
  9.4 156.1 %all-gather.7.cloned.1.call-start = ((), (), s32[]{:S(2)}) async-start(), calls=%async_computation.10 | async-start | bytes 4456448 | tf_op jit(solution)/shard_map/all_gather | solution.py:263
  10.1 201.9 %reduce-scatter.14.cloned.1.call-start = ((), (), s32[]{:S(2)}) async-start(), calls=%async_computation.15 | async-start | bytes 3145728 | tf_op jit(solution)/shard_map/reduce_scatter | solution.py:43
  10.9 15.9 collective-permute-start
  13.9 23.3 collective-permute-start.2
  170.4 76.2 %reduce-scatter.10.cloned.1.call-start = ((), (), s32[]{:S(2)}) async-start(), calls=%async_computation.11 | async-start | bytes 3145728 | tf_op jit(solution)/shard_map/reduce_scatter | solution.py:43
  178.3 238.4 %all-gather.9.cloned.1.call-start = ((), (), s32[]{:S(2)}) async-start(), calls=%async_computation.12 | async-start | bytes 35651584 | tf_op jit(solution)/shard_map/all_gather | solution.py:264
  181.3 363.9 %all-gather.11.cloned.1.call-start = ((), (), s32[]{:S(2)}) async-start(), calls=%async_computation.13 | async-start | bytes 17825792 | tf_op jit(solution)/shard_map/all_gather | solution.py:265
  181.9 435.3 %reduce-scatter.18.cloned.1.call-start = ((), (), s32[]{:S(2)}) async-start(), calls=%async_computation.17 | async-start | bytes 3145728 | tf_op jit(solution)/shard_map/reduce_scatter | solution.py:43
  183.6 65.6 %collective-permute-start.4 = (bf16[1,128,2048]{2,1,0:T(8,128)(2,1)}, bf16[1,128,2048]{2,1,0:T(8,128)(2,1)}, u32[]{:S(2)}, u32[]{:S(2)}) collective-permute-start(bf16[1,128,2048]{2,1,0:T(8,128)(2,1)} %get-tuple-element.142), channel_id=1, source_target_pairs={{0,1},{1,0},{2,3},{3,2},{4,5},{5,4},{6,7},{7,6},{8,9},{9,8},{10,11... | collective-permute-start | bytes 1572872 | tf_op jit(solution)/shard_map/ppermute | solution.py:29
  248.5 501.3 %copy-start = (f32[1,128,2048]{2,1,0:T(8,128)}, f32[1,128,2048]{2,1,0:T(8,128)S(1)}, u32[]{:S(2)}) copy-start(f32[1,128,2048]{2,1,0:T(8,128)S(1)} %get-tuple-element.147) | copy-start | bytes 3145732
  248.5 501.3 %copy-start.2 = (f32[1,128,2048]{2,1,0:T(8,128)}, f32[1,128,2048]{2,1,0:T(8,128)S(1)}, u32[]{:S(2)}) copy-start(f32[1,128,2048]{2,1,0:T(8,128)S(1)} %get-tuple-element.105) | copy-start | bytes 3145732
  248.6 501.3 %copy-start.103 = (f32[128]{0:T(128)}, f32[128]{0:T(128)S(1)}, u32[]{:S(2)}) copy-start(f32[128]{0:T(128)S(1)} %add_rsqrt_fusion.2) | copy-start | bytes 1540
  248.7 13.6 collective-permute-start.1
  578.1 137.5 %reduce-scatter.22.cloned.1.call-start = ((), (), s32[]{:S(2)}) async-start(), calls=%async_computation.19 | async-start | bytes 3145728 | tf_op jit(solution)/shard_map/reduce_scatter | solution.py:43
  579.2 41.7 %collective-permute-start.6 = (bf16[1,128,2048]{2,1,0:T(8,128)(2,1)S(1)}, bf16[1,128,2048]{2,1,0:T(8,128)(2,1)S(1)}, u32[]{:S(2)}, u32[]{:S(2)}) collective-permute-start(bf16[1,128,2048]{2,1,0:T(8,128)(2,1)S(1)} %copy-done.67), channel_id=1, source_target_pairs={{0,1},{1,0},{2,3},{3,2},{4,5},{5,4},{6,7},{7,6},{8,9},{9,8},{10,11... | collective-permute-start | bytes 1572872 | tf_op jit(solution)/shard_map/ppermute | solution.py:29
  619.4 13.8 collective-permute-start.3
  685.4 64.4 %reduce-scatter.16.cloned.1.call-start = ((), (), s32[]{:S(2)}) async-start(), calls=%async_computation.16 | async-start | bytes 3145728 | tf_op jit(solution)/shard_map/reduce_scatter | solution.py:43
  698.6 383.3 %reduce-scatter.24.cloned.1.call-start = ((), (), s32[]{:S(2)}) async-start(), calls=%async_computation.20 | async-start | bytes 3145728 | tf_op jit(solution)/shard_map/reduce_scatter | solution.py:43
  753.4 15.8 collective-permute-start.7
  767.5 15.6 collective-permute-start.5
  820.6 261.3 %reduce-scatter.20.cloned.1.call-start = ((), (), s32[]{:S(2)}) async-start(), calls=%async_computation.18 | async-start | bytes 3145728 | tf_op jit(solution)/shard_map/reduce_scatter | solution.py:43
  845.6 278.8 %reduce-scatter.12.cloned.1.call-start = ((), (), s32[]{:S(2)}) async-start(), calls=%async_computation.14 | async-start | bytes 3145728 | tf_op jit(solution)/shard_map/reduce_scatter | solution.py:43
  883.7 1435.6 %reduce-scatter.26.cloned.1.call-start = ((), (), s32[]{:S(2)}) async-start(), calls=%async_computation.21 | async-start | bytes 142606336 | tf_op jit(solution)/shard_map/reduce_scatter | solution.py:290
  (129 other events, 1978.0 us)
Sparse Core Ops, SparseCore 0:
  10.9 103.1 all-gather.4
  116.2 48.6 all-gather.6
  170.5 41.4 reduce-scatter.13
  214.7 31.8 reduce-scatter.9
  248.7 168.0 all-gather.8
  418.8 126.4 all-gather.10
  578.3 38.9 reduce-scatter.17
  685.5 30.0 reduce-scatter.21
  717.9 31.9 reduce-scatter.15
  820.7 31.8 reduce-scatter.23
  854.9 31.8 reduce-scatter.19
  888.9 31.8 reduce-scatter.11
  1081.3 1238.0 reduce-scatter.25
